TPU v7x, 32 devices: a whole 2x2x4 slice. The times are simulated.
32 devices in a mesh: dp: 8 (over z, y), tensor: 4 (over x, core).
Axes of the slice: x: 2, y: 2, z: 4, core: 2. Of those that a mesh axis runs over, the one named last changes fastest.
Arguments:
- tokens: bfloat16 [16384, 768], P(('dp', 'tensor')), may hold values from -6 to 6
- gene_counts: int32 [16], P('dp'), may hold values from 300 to 1024, as said below
- in_proj: bfloat16 [3, 768, 768], P(None, None, 'tensor'), may hold values from -0.21875 to 0.21875
- out_proj: bfloat16 [768, 768], P('tensor'), may hold values from -0.875 to 0.875
- up_proj: bfloat16 [768, 3072], P(None, 'tensor'), may hold values from -0.21875 to 0.21875
- down_proj: bfloat16 [3072, 768], P('tensor'), may hold values from -0.109375 to 0.109375
- gains: float32 [2, 768], replicated, may hold values from 0.1 to 1.9
- biases: float32 [2, 768], replicated, may hold values from -3 to 3
- cotangent: bfloat16 [16384, 768], P(('dp', 'tensor')), may hold values from -6 to 6
Outputs:
- block_out: bfloat16 [16384, 768], P(('dp', 'tensor'))
- input_grad: bfloat16 [16384, 768], P(('dp', 'tensor'))
- grad_in_proj: float32 [3, 768, 768], P(None, 'dp', 'tensor')
- grad_out_proj: float32 [768, 768], P('tensor', 'dp')
- grad_up_proj: float32 [768, 3072], P('dp', 'tensor')
- grad_down_proj: float32 [3072, 768], P('tensor', 'dp')
- grad_gains: float32 [2, 768], replicated
- grad_biases: float32 [2, 768], replicated
Inputs may be any that keep to these rules, and one draw needn't show every extreme that they name: Cell c holds genes at its first gene_counts[c] positions and padding at the rest of its 1024 positions; in every draw one cell holds 1024 genes and one holds 300; most cells are short.
All inputs are finite; a program needn't handle non-finite values.
Results may differ from a plain program's by a relative error of at most 0.013.
The roundings to bfloat16 on the way count: a program that leaves them out, or rounds other values in their place, can miss the bound.
Values may be sent and summed in bfloat16 or wider, within the bound.
A program may use at most 128 MiB of HBM per device.

v0:
```python
import jax
import jax.numpy as jnp
from jax import lax
from jax.sharding import PartitionSpec as P

HEAD_DIM = 64
EPS = 1e-05
NEG = -1e30


def layer_norm(values, gain, offset):
    center = values - jnp.mean(values, axis=-1, keepdims=True)
    spread = jnp.mean(center * center, axis=-1, keepdims=True)
    return center * lax.rsqrt(spread + EPS) * gain + offset


def gelu_exact(values):
    return jax.nn.gelu(values, approximate=False)


def per_device(
    tokens, gene_counts, in_proj, out_proj, up_proj, down_proj, gains, biases, cotangent
):
    rows = tokens.shape[0]
    cells = gene_counts.shape[0]
    group = rows * lax.axis_size("tensor")
    length = group // cells
    local_width = out_proj.shape[0]
    heads = local_width // HEAD_DIM
    block = min(length, 512)
    blocks = length // block
    scale = HEAD_DIM ** (-0.5)
    positions = jnp.arange(length, dtype=jnp.int32)
    resid = tokens.astype(jnp.float32)
    normed, first_back = jax.vjp(layer_norm, resid, gains[0], biases[0])
    normed_all = lax.all_gather(normed.astype(jnp.bfloat16), "tensor", axis=0, tiled=True)
    projected = jnp.einsum(
        "td,cde->cte", normed_all, in_proj, preferred_element_type=jnp.float32
    ).astype(jnp.bfloat16)
    query_cells = projected[0].reshape(cells, blocks, block, local_width)
    key_cells = projected[1].reshape(cells, length, local_width)
    value_cells = projected[2].reshape(cells, length, local_width)

    def block_scores(query_block, key_rows, count):
        query_heads = query_block.reshape(block, heads, HEAD_DIM)
        key_heads = key_rows.reshape(length, heads, HEAD_DIM)
        scores = (
            jnp.einsum("qhd,khd->hqk", query_heads, key_heads, preferred_element_type=jnp.float32)
            * scale
        )
        return jnp.where((positions < count)[None, None, :], scores, NEG)

    def cell_forward(item):
        queries, key_rows, value_rows, count = item
        value_heads = value_rows.reshape(length, heads, HEAD_DIM)

        def one_block(query_block):
            scores = block_scores(query_block, key_rows, count)
            top = jnp.max(scores, axis=-1, keepdims=True)
            expo = jnp.exp(scores - top)
            total = jnp.sum(expo, axis=-1, keepdims=True)
            probs = (expo / total).astype(jnp.bfloat16)
            result = jnp.einsum(
                "hqk,khd->qhd", probs, value_heads, preferred_element_type=jnp.float32
            )
            return (
                result.reshape(block, local_width).astype(jnp.bfloat16),
                (top + jnp.log(total))[..., 0],
            )

        return lax.map(one_block, queries)

    attended, log_totals = lax.map(cell_forward, (query_cells, key_cells, value_cells, gene_counts))
    attended = attended.reshape(group, local_width)
    piece = attended
    mid = resid + lax.psum_scatter(
        jnp.dot(piece, out_proj, preferred_element_type=jnp.float32),
        "tensor",
        scatter_dimension=0,
        tiled=True,
    )
    normed_mid, second_back = jax.vjp(layer_norm, mid, gains[1], biases[1])
    mid_low = normed_mid.astype(jnp.bfloat16)
    mid_all = lax.all_gather(mid_low, "tensor", axis=0, tiled=True)
    hidden = jnp.dot(mid_all, up_proj, preferred_element_type=jnp.float32)
    active = gelu_exact(hidden).astype(jnp.bfloat16)
    piece = active
    block_out = (
        mid
        + lax.psum_scatter(
            jnp.dot(piece, down_proj, preferred_element_type=jnp.float32).astype(jnp.bfloat16),
            "tensor",
            scatter_dimension=0,
            tiled=True,
        ).astype(jnp.float32)
    ).astype(jnp.bfloat16)
    out_grads = lax.all_gather(cotangent, "tensor", axis=0, tiled=True)
    _, gelu_back = jax.vjp(gelu_exact, hidden)
    active_grad = jnp.einsum("td,fd->tf", out_grads, down_proj, preferred_element_type=jnp.float32)
    hidden_grad = gelu_back(active_grad)[0].astype(jnp.bfloat16)
    grad_down = jnp.einsum("tf,td->fd", active, out_grads, preferred_element_type=jnp.float32)
    grad_up = jnp.einsum("td,tf->df", mid_all, hidden_grad, preferred_element_type=jnp.float32)
    piece = hidden_grad
    mid_grad = lax.psum_scatter(
        jnp.einsum("tf,df->td", piece, up_proj, preferred_element_type=jnp.float32),
        "tensor",
        scatter_dimension=0,
        tiled=True,
    )
    resid_part, gain_second, bias_second = second_back(mid_grad)
    mid_total = cotangent.astype(jnp.float32) + resid_part
    branch_all = lax.all_gather(mid_total.astype(jnp.bfloat16), "tensor", axis=0, tiled=True)
    attended_grad = jnp.einsum(
        "td,ed->te", branch_all, out_proj, preferred_element_type=jnp.float32
    ).astype(jnp.bfloat16)
    grad_out = jnp.einsum("te,td->ed", attended, branch_all, preferred_element_type=jnp.float32)

    def cell_backward(item):
        queries, key_rows, value_rows, count, grad_rows, totals = item
        key_heads = key_rows.reshape(length, heads, HEAD_DIM)
        value_heads = value_rows.reshape(length, heads, HEAD_DIM)

        def one_block(carry, part):
            key_sum, value_sum = carry
            query_block, grad_block, total_block = part
            scores = block_scores(query_block, key_rows, count)
            probs = jnp.exp(scores - total_block[..., None])
            grad_heads = grad_block.reshape(block, heads, HEAD_DIM)
            query_heads = query_block.reshape(block, heads, HEAD_DIM)
            prob_grads = jnp.einsum(
                "qhd,khd->hqk", grad_heads, value_heads, preferred_element_type=jnp.float32
            )
            inner = jnp.sum(probs * prob_grads, axis=-1, keepdims=True)
            score_grads = (probs * (prob_grads - inner)).astype(jnp.bfloat16)
            query_grad = (
                jnp.einsum(
                    "hqk,khd->qhd", score_grads, key_heads, preferred_element_type=jnp.float32
                )
                * scale
            )
            key_sum = (
                key_sum
                + jnp.einsum(
                    "hqk,qhd->khd", score_grads, query_heads, preferred_element_type=jnp.float32
                )
                * scale
            )
            value_sum = value_sum + jnp.einsum(
                "hqk,qhd->khd",
                probs.astype(jnp.bfloat16),
                grad_heads,
                preferred_element_type=jnp.float32,
            )
            return (
                (key_sum, value_sum),
                query_grad.reshape(block, local_width).astype(jnp.bfloat16),
            )

        zeros = jnp.zeros((length, heads, HEAD_DIM), jnp.float32)
        (key_sum, value_sum), query_grads = lax.scan(
            one_block, (zeros, zeros), (queries, grad_rows, totals)
        )
        return (
            query_grads.reshape(length, local_width),
            key_sum.reshape(length, local_width).astype(jnp.bfloat16),
            value_sum.reshape(length, local_width).astype(jnp.bfloat16),
        )

    grad_cells = attended_grad.reshape(cells, blocks, block, local_width)
    query_grads, key_grads, value_grads = lax.map(
        cell_backward, (query_cells, key_cells, value_cells, gene_counts, grad_cells, log_totals)
    )
    proj_grads = jnp.stack(
        [
            query_grads.reshape(group, local_width),
            key_grads.reshape(group, local_width),
            value_grads.reshape(group, local_width),
        ]
    )
    grad_in = jnp.einsum("td,cte->cde", normed_all, proj_grads, preferred_element_type=jnp.float32)
    piece = proj_grads
    normed_grad = lax.psum_scatter(
        jnp.einsum("cte,cde->td", piece, in_proj, preferred_element_type=jnp.float32),
        "tensor",
        scatter_dimension=0,
        tiled=True,
    )
    resid_grad, gain_first, bias_first = first_back(normed_grad)
    input_grad = (mid_total + resid_grad).astype(jnp.bfloat16)
    grad_gains, grad_biases = lax.psum(
        (jnp.stack([gain_first, gain_second]), jnp.stack([bias_first, bias_second])),
        ("dp", "tensor"),
    )
    grad_in_part, grad_out_part, grad_up_part, grad_down_part = (
        lax.psum_scatter(grad_in, "dp", scatter_dimension=1, tiled=True),
        lax.psum_scatter(grad_out, "dp", scatter_dimension=1, tiled=True),
        lax.psum_scatter(grad_up, "dp", scatter_dimension=0, tiled=True),
        lax.psum_scatter(grad_down, "dp", scatter_dimension=1, tiled=True),
    )
    return (
        block_out,
        input_grad,
        grad_in_part,
        grad_out_part,
        grad_up_part,
        grad_down_part,
        grad_gains,
        grad_biases,
    )


def solution(mesh):
    placed = (
        P(("dp", "tensor"), None),
        P("dp"),
        P(None, None, "tensor"),
        P("tensor", None),
        P(None, "tensor"),
        P("tensor", None),
        P(),
        P(),
        P(("dp", "tensor"), None),
    )
    return jax.shard_map(
        per_device,
        mesh=mesh,
        in_specs=placed,
        out_specs=(
            P(("dp", "tensor"), None),
            P(("dp", "tensor"), None),
            P(None, "dp", "tensor"),
            P("tensor", "dp"),
            P("dp", "tensor"),
            P("tensor", "dp"),
            P(),
            P(),
        ),
        check_vma=False,
    )
```

profile of v0, /device:TPU:0, one launch (start us, length us, event | category | flops | bytes accessed | tf_op | source)
XLA Modules:
  0.0 751.3 jit_solution(6833605343567260367)
XLA Ops:
  12.2 2.4 fusion.40
  14.6 31.3 %all-gather.5.cloned.1.call-done = bf16[2048,768]{1,0:T(8,128)(2,1)} async-done(((bf16[512,768]{1,0:T(8,128)(2,1)}), bf16[2048,768]{1,0:T(8,128)(2,1)}) %all-gather.5.cloned.1.call-update) | async-done | bytes 3145744 | tf_op jit(solution)/shard_map/all_gather | solution.py:36
  45.9 3.9 fusion.59
  51.9 2.2 copy.49
  55.7 40.2 %while.58 = (s32[]{:T(128)}, bf16[2,2,512,192]{2,1,0,3:T(2,128)(2,1)}, f32[2,2,3,512]{3,2,1,0:T(4,128)}, bf16[2,2,512,192]{2,3,1,0:T(8,128)(2,1)S(1)}, bf16[2,10...) while((s32[]{:T(128)}, ...), condition=%wide.region_7.8_spmd.clone, body=%wide.region_2.7_spmd.clone.sunk | while | flops 421625344 | bytes 28903900 | solution.py:73
  56.9 1.8 constant_dynamic-slice_fusion.13
  58.8 13.5 %while.61 = (s32[]{:T(128)}, bf16[2,512,192]{1,2,0:T(8,128)(2,1)}, f32[2,3,512]{2,1,0:T(4,128)}, s32[]{:T(128)}, s32[1024]{0:T(1024)S(1)}, /*index=5*/bf16[2,512...) while((s32[]{:T(128)}, bf16[2,512,192]{1,2,0:T(8,128)(2,1)}, ...), condition=%wide.region_6.6_spmd, body=%wide.region_3.5_spmd.sunk | while | flops 421625344 | bytes 25721088 | solution.py:71
  62.2 2.0 fusion.140
  67.3 1.6 fusion.139
  68.9 2.0 fusion.140
  73.6 2.1 copy_dynamic-update-slice_fusion.2
  77.0 1.8 constant_dynamic-slice_fusion.13
  78.9 13.5 %while.61 = (s32[]{:T(128)}, bf16[2,512,192]{1,2,0:T(8,128)(2,1)}, f32[2,3,512]{2,1,0:T(4,128)}, s32[]{:T(128)}, s32[1024]{0:T(1024)S(1)}, /*index=5*/bf16[2,512...) while((s32[]{:T(128)}, bf16[2,512,192]{1,2,0:T(8,128)(2,1)}, ...), condition=%wide.region_6.6_spmd, body=%wide.region_3.5_spmd.sunk | while | flops 421625344 | bytes 25721088 | solution.py:71
  82.2 2.0 fusion.140
  87.4 1.6 fusion.139
  89.0 2.0 fusion.140
  93.7 2.1 copy_dynamic-update-slice_fusion.2
  95.9 2.8 reshape.203
  98.7 4.9 fusion.60
  103.8 58.3 %reduce-scatter.13.cloned.1.call-done = f32[512,768]{1,0:T(8,128)} async-done(((f32[2048,768]{1,0:T(8,128)}), f32[512,768]{1,0:T(8,128)}) %reduce-scatter.13.cloned.1.call-update) | async-done | bytes 1572880 | tf_op jit(solution)/shard_map/reduce_scatter | solution.py:76
  162.1 1.8 fusion.56
  164.3 1.9 add_convert_fusion.3
  166.8 28.1 %all-gather.7.cloned.1.call-done = bf16[2048,768]{1,0:T(8,128)(2,1)} async-done(((bf16[512,768]{1,0:T(8,128)(2,1)}), bf16[2048,768]{1,0:T(8,128)(2,1)}) %all-gather.7.cloned.1.call-update) | async-done | bytes 3145744 | tf_op jit(solution)/shard_map/all_gather | solution.py:84
  194.9 7.5 fusion.61
  202.3 22.6 %all-gather.9.cloned.1.call-done = bf16[2048,768]{1,0:T(8,128)(2,1)} async-done(((bf16[512,768]{1,0:T(8,128)(2,1)}), bf16[2048,768]{1,0:T(8,128)(2,1)}) %all-gather.9.cloned.1.call-update) | async-done | bytes 3145744 | tf_op jit(solution)/shard_map/all_gather | solution.py:97
  224.9 19.2 %add_convert_fusion = (bf16[2048,768]{1,0:T(8,128)(2,1)S(1)}, f32[2048,768]{1,0:T(8,128)}) fusion(f32[2048,768]{1,0:T(8,128)} %fusion.61, bf16[2048,768]{1,0:T(8,128)(2,1)} %all-gather.9.cloned.1.call-done, bf16[768,768]{1,0:T(8,128)(2,1)S(1)} %copy-done), kind=kOutput, calls=%fused_computation.51 | convolution fusion | flops 2529165312 | bytes 20054016 | tf_op jit(solution)/shard_map/td,fd->tf/dot_general | solution.py:99
  244.1 1.7 copy-done.44
  245.8 4.5 fusion.62
  250.4 5.5 multiply_convert_fusion.1
  255.9 1.7 copy-done.18
  257.6 4.0 convolution_convert_fusion
  261.9 47.0 %reduce-scatter.17.cloned.1.call-done = f32[512,768]{1,0:T(8,128)} async-done(((f32[2048,768]{1,0:T(8,128)}), f32[512,768]{1,0:T(8,128)}) %reduce-scatter.17.cloned.1.call-update) | async-done | bytes 1572880 | tf_op jit(solution)/shard_map/reduce_scatter | solution.py:104
  308.9 2.6 multiply_reduce_fusion.1
  311.5 37.8 %reduce-scatter.15.cloned.1.call-done = bf16[512,768]{1,0:T(8,128)(2,1)} async-done(((bf16[2048,768]{1,0:T(8,128)(2,1)}), bf16[512,768]{1,0:T(8,128)(2,1)}) %reduce-scatter.15.cloned.1.call-update) | async-done | bytes 786448 | tf_op jit(solution)/shard_map/reduce_scatter | solution.py:90
  349.3 3.1 fusion.54
  354.9 28.6 %all-gather.11.cloned.1.call-done = bf16[2048,768]{1,0:T(8,128)(2,1)} async-done(((bf16[512,768]{1,0:T(8,128)(2,1)}), bf16[2048,768]{1,0:T(8,128)(2,1)}) %all-gather.11.cloned.1.call-update) | async-done | bytes 3145744 | tf_op jit(solution)/shard_map/all_gather | solution.py:112
  383.5 3.1 convolution_convert_fusion.1
  387.1 4.1 convolution_bitcast_fusion.1
  391.3 62.7 %while.60 = (s32[]{:T(128)}, bf16[2,1024,192]{2,1,0:T(8,128)(2,1)}, bf16[2,1024,192]{1,2,0:T(8,128)(2,1)}, bf16[2,1024,192]{1,2,0:T(8,128)(2,1)}, bf16[2,2,512,1...) while((s32[]{:T(128)}, bf16[2,1024,192]{2,1,0:T(8,128)(2,1)}, ...), condition=%wide.region_19.20_spmd.clone, body=%wide.region_15.19_spmd.clone.sunk | while | flops 1031798272 | bytes 92420848 | solution.py:170
  396.5 21.5 %while.62 = (s32[]{:T(128)}, f32[1024,3,64]{0,2,1:T(8,128)S(1)}, f32[1024,3,64]{0,2,1:T(8,128)}, bf16[2,512,192]{1,2,0:T(8,128)(2,1)}, bf16[2,512,192]{1,2,0:T(8...) while((s32[]{:T(128)}, f32[1024,3,64]{0,2,1:T(8,128)S(1)}, ...), condition=%wide.region_18.18_spmd.clone, body=%wide.region_16.17_spmd.clone.sunk | while | flops 1031405056 | bytes 63162644 | solution.py:160
  400.6 2.1 multiply_reduce_fusion.5
  402.7 1.7 multiply_convert_fusion.3
  411.3 2.1 multiply_reduce_fusion.5
  413.4 1.7 multiply_convert_fusion.3
  427.8 21.5 %while.62 = (s32[]{:T(128)}, f32[1024,3,64]{0,2,1:T(8,128)S(1)}, f32[1024,3,64]{0,2,1:T(8,128)}, bf16[2,512,192]{1,2,0:T(8,128)(2,1)}, bf16[2,512,192]{1,2,0:T(8...) while((s32[]{:T(128)}, f32[1024,3,64]{0,2,1:T(8,128)S(1)}, ...), condition=%wide.region_18.18_spmd.clone, body=%wide.region_16.17_spmd.clone.sunk | while | flops 1031405056 | bytes 63162644 | solution.py:160
  431.9 2.1 multiply_reduce_fusion.5
  434.0 1.7 multiply_convert_fusion.3
  442.7 2.1 multiply_reduce_fusion.5
  444.7 1.7 multiply_convert_fusion.3
  454.0 2.1 copy.59
  459.9 4.1 fusion.44
  464.1 2.7 copy.62
  466.8 4.8 reshape.219
  471.7 4.6 convolution_bitcast_fusion
  476.3 7.0 fusion.64
  483.6 7.0 fusion.63
  491.9 1.6 copy.65
  493.5 45.0 %reduce-scatter.25.cloned.1.call-done = f32[96,576]{1,0:T(8,128)} async-done(((f32[768,576]{1,0:T(8,128)}), f32[96,576]{1,0:T(8,128)}) %reduce-scatter.25.cloned.1.call-update) | async-done | bytes 221200
  540.4 58.0 %reduce-scatter.19.cloned.1.call-done = f32[512,768]{1,0:T(8,128)} async-done(((f32[2048,768]{1,0:T(8,128)}), f32[512,768]{1,0:T(8,128)}) %reduce-scatter.19.cloned.1.call-update) | async-done | bytes 1572880 | tf_op jit(solution)/shard_map/reduce_scatter | solution.py:182
  598.5 2.0 fusion.53
  604.4 40.3 %all-reduce = (f32[2,768]{1,0:T(2,128)}, f32[2,768]{1,0:T(2,128)}) all-reduce(f32[2,768]{1,0:T(2,128)} %pad_maximum_fusion.3, f32[2,768]{1,0:T(2,128)} %pad_maximum_fusion.4), channel_id=1, replica_groups=mesh['dp'=8,'tensor'=4] {'dp','tensor'}, use_global_device_ids=true, to_apply=%region_29.30 | all-reduce | flops 3072 | bytes 24576 | tf_op jit(solution)/shard_map/psum | solution.py:190
  645.4 3.2 add_convert_fusion.1
  648.6 23.5 %reduce-scatter.23.cloned.1.call-done = f32[768,96]{0,1:T(8,128)} async-done(((f32[768,768]{0,1:T(8,128)}), f32[768,96]{0,1:T(8,128)}) %reduce-scatter.23.cloned.1.call-update) | async-done | bytes 294928 | tf_op jit(solution)/shard_map/reduce_scatter | solution.py:198
  672.1 72.2 %reduce-scatter.21.cloned.1.call-done = f32[96,768]{1,0:T(8,128)} async-done(((f32[768,768]{1,0:T(8,128)}), f32[96,768]{1,0:T(8,128)}) %reduce-scatter.21.cloned.1.call-update) | async-done | bytes 294928 | tf_op jit(solution)/shard_map/reduce_scatter | solution.py:197
  (320 shorter events, 92.7 us)
Async XLA Ops:
  7.2 217.7 %copy-start = (bf16[768,768]{1,0:T(8,128)(2,1)S(1)}, bf16[768,768]{1,0:T(8,128)(2,1)}, u32[]{:S(2)}) copy-start(bf16[768,768]{1,0:T(8,128)(2,1)} %param.22) | copy-start | bytes 3538948
  7.2 38.8 %copy-start.42 = (bf16[3,768,192]{1,2,0:T(8,128)(2,1)S(1)}, bf16[3,768,192]{1,2,0:T(8,128)(2,1)}, u32[]{:S(2)}) copy-start(bf16[3,768,192]{1,2,0:T(8,128)(2,1)} %param.19) | copy-start | bytes 2654212
  7.2 38.7 %all-gather.5.cloned.1.call-start = ((), (), s32[]{:S(2)}) async-start(), calls=%async_computation.8 | async-start | bytes 3932160 | tf_op jit(solution)/shard_map/all_gather | solution.py:36
  8.7 41.2 %copy-start.31 = (f32[512]{0:T(512)}, f32[512]{0:T(512)S(1)}, u32[]{:S(2)}) copy-start(f32[512]{0:T(512)S(1)} %broadcast_multiply_fusion.1) | copy-start | bytes 6148
  10.8 39.1 %copy-start.34 = (f32[512]{0:T(512)}, f32[512]{0:T(512)S(1)}, u32[]{:S(2)}) copy-start(f32[512]{0:T(512)S(1)} %fusion.48) | copy-start | bytes 6148
  12.2 37.7 %copy-start.29 = (f32[768]{0:T(1024)}, f32[768]{0:T(1024)S(1)}, u32[]{:S(2)}) copy-start(f32[768]{0:T(1024)S(1)} %get-tuple-element.496) | copy-start | bytes 9220
  14.6 147.5 %reduce-scatter.13.cloned.1.call-start = ((), (), s32[]{:S(2)}) async-start(), calls=%async_computation.9 | async-start | bytes 7864320 | tf_op jit(solution)/shard_map/reduce_scatter | solution.py:76
  60.5 1.6 copy-start.10
  62.1 2.0 copy-start.26
  62.1 2.1 copy-start.11
  67.3 1.6 copy-start.10
  68.9 2.0 copy-start.26
  68.9 2.1 copy-start.11
  80.6 1.6 copy-start.10
  82.2 2.0 copy-start.26
  82.2 2.1 copy-start.11
  87.4 1.6 copy-start.10
  89.0 2.0 copy-start.26
  89.0 2.1 copy-start.11
  95.9 7.7 %copy-start.3 = (bf16[2,2,512,192]{2,3,1,0:T(8,128)(2,1)}, bf16[2,2,512,192]{2,3,1,0:T(8,128)(2,1)S(1)}, u32[]{:S(2)}) copy-start(bf16[2,2,512,192]{2,3,1,0:T(8,128)(2,1)S(1)} %get-tuple-element.948) | copy-start | bytes 2359300
  98.7 4.9 copy-start.16
  103.6 60.7 %copy-start.33 = (f32[768]{0:T(1024)S(1)}, f32[768]{0:T(1024)}, u32[]{:S(2)}) copy-start(f32[768]{0:T(1024)} %get-tuple-element.497) | copy-start | bytes 9220
  103.6 91.3 %all-gather.7.cloned.1.call-start = ((), (), s32[]{:S(2)}) async-start(), calls=%async_computation.10 | async-start | bytes 3932160 | tf_op jit(solution)/shard_map/all_gather | solution.py:84
  166.2 58.8 %all-gather.9.cloned.1.call-start = ((), (), s32[]{:S(2)}) async-start(), calls=%async_computation.12 | async-start | bytes 3932160 | tf_op jit(solution)/shard_map/all_gather | solution.py:97
  166.7 142.1 %reduce-scatter.17.cloned.1.call-start = ((), (), s32[]{:S(2)}) async-start(), calls=%async_computation.13 | async-start | bytes 7864320 | tf_op jit(solution)/shard_map/reduce_scatter | solution.py:104
  224.9 20.9 %copy-start.41 = (bf16[768,768]{1,0:T(8,128)(2,1)S(1)}, bf16[768,768]{1,0:T(8,128)(2,1)}, u32[]{:S(2)}) copy-start(bf16[768,768]{1,0:T(8,128)(2,1)} %param.21) | copy-start | bytes 3538948
  244.1 1.7 copy-start.44
  250.4 98.9 %reduce-scatter.15.cloned.1.call-start = ((), (), s32[]{:S(2)}) async-start(), calls=%async_computation.11 | async-start | bytes 3932160 | tf_op jit(solution)/shard_map/reduce_scatter | solution.py:90
  255.9 1.7 copy-start.18
  261.6 121.9 %all-gather.11.cloned.1.call-start = ((), (), s32[]{:S(2)}) async-start(), calls=%async_computation.14 | async-start | bytes 3932160 | tf_op jit(solution)/shard_map/all_gather | solution.py:112
  311.5 42.1 %copy-start.15 = (bf16[512,768]{1,0:T(8,128)(2,1)S(1)}, bf16[512,768]{1,0:T(8,128)(2,1)}, u32[]{:S(2)}) copy-start(bf16[512,768]{1,0:T(8,128)(2,1)} %param.25) | copy-start | bytes 2359300
  352.4 31.1 %copy-start.28 = (bf16[192,768]{1,0:T(8,128)(2,1)S(1)}, bf16[192,768]{1,0:T(8,128)(2,1)}, u32[]{:S(2)}) copy-start(bf16[192,768]{1,0:T(8,128)(2,1)} %param.20) | copy-start | bytes 884740
  352.4 34.1 %copy-start.38 = (f32[512]{0:T(512)}, f32[512]{0:T(512)S(1)}, u32[]{:S(2)}) copy-start(f32[512]{0:T(512)S(1)} %negate_multiply_fusion.2) | copy-start | bytes 6148
  354.8 137.1 %reduce-scatter.27.cloned.1.call-start = ((), (), s32[]{:S(2)}) async-start(), calls=%async_computation.19 | async-start | bytes 884736
  354.9 32.3 %copy-start.17 = (bf16[2048,192]{0,1:T(8,128)(2,1)S(1)}, bf16[2048,192]{0,1:T(8,128)(2,1)}, u32[]{:S(2)}) copy-start(bf16[2048,192]{0,1:T(8,128)(2,1)} %copy-done.16) | copy-start | bytes 2359300
  391.3 147.3 %reduce-scatter.25.cloned.1.call-start = ((), (), s32[]{:S(2)}) async-start(), calls=%async_computation.18 | async-start | bytes 2211840
  391.4 5.1 copy-start.13
  400.6 2.1 copy-start.5
  411.3 2.1 copy-start.5
  418.0 3.5 copy-start.20
  419.3 2.2 copy-start.22
  419.3 3.4 copy-start.14
  422.7 5.1 copy-start.13
  431.9 2.1 copy-start.5
  442.6 2.1 copy-start.5
  449.3 3.5 copy-start.20
  450.6 2.2 copy-start.22
  450.7 3.4 copy-start.14
  454.0 3.6 copy-start.19
  454.0 4.5 copy-start.24
  466.8 4.9 copy-start.25
  466.8 4.9 copy-start.43
  471.6 126.8 %reduce-scatter.19.cloned.1.call-start = ((), (), s32[]{:S(2)}) async-start(), calls=%async_computation.15 | async-start | bytes 7864320 | tf_op jit(solution)/shard_map/reduce_scatter | solution.py:182
  476.3 195.8 %reduce-scatter.23.cloned.1.call-start = ((), (), s32[]{:S(2)}) async-start(), calls=%async_computation.17 | async-start | bytes 2654208 | tf_op jit(solution)/shard_map/reduce_scatter | solution.py:198
  483.4 7.3 copy-start.40
  483.4 7.9 %copy-start.39 = (f32[768]{0:T(1024)S(1)}, f32[768]{0:T(1024)}, u32[]{:S(2)}) copy-start(f32[768]{0:T(1024)} %get-tuple-element.397) | copy-start | bytes 9220
  483.4 260.9 %reduce-scatter.21.cloned.1.call-start = ((), (), s32[]{:S(2)}) async-start(), calls=%async_computation.16 | async-start | bytes 2654208 | tf_op jit(solution)/shard_map/reduce_scatter | solution.py:197
  490.6 107.8 %copy-start.2 = (bf16[512,768]{1,0:T(8,128)(2,1)S(1)}, bf16[512,768]{1,0:T(8,128)(2,1)}, u32[]{:S(2)}) copy-start(bf16[512,768]{1,0:T(8,128)(2,1)} %param.17) | copy-start | bytes 2359300
  490.6 107.8 %copy-start.30 = (f32[768]{0:T(1024)S(1)}, f32[768]{0:T(1024)}, u32[]{:S(2)}) copy-start(f32[768]{0:T(1024)} %copy-done.29) | copy-start | bytes 9220
  490.7 107.8 %copy-start.32 = (f32[512]{0:T(512)S(1)}, f32[512]{0:T(512)}, u32[]{:S(2)}) copy-start(f32[512]{0:T(512)} %copy-done.31) | copy-start | bytes 6148
  490.7 109.8 %copy-start.37 = (f32[512]{0:T(512)S(1)}, f32[512]{0:T(512)}, u32[]{:S(2)}) copy-start(f32[512]{0:T(512)} %copy-done.36) | copy-start | bytes 6148
  490.7 109.8 %copy-start.35 = (f32[512]{0:T(512)S(1)}, f32[512]{0:T(512)}, u32[]{:S(2)}) copy-start(f32[512]{0:T(512)} %copy-done.34) | copy-start | bytes 6148
  598.5 2.0 copy-start.6
  600.5 143.8 %copy-start.1 = (bf16[768,768]{1,0:T(8,128)(2,1)S(1)}, bf16[768,768]{1,0:T(8,128)(2,1)}, u32[]{:S(2)}) copy-start(bf16[768,768]{1,0:T(8,128)(2,1)} %param.22) | copy-start | bytes 3538948
  (26 other events, 22.8 us)
Sparse Core Ops, SparseCore 0:
  14.7 31.2 all-gather.4
  103.7 58.3 reduce-scatter.12
  166.3 28.5 all-gather.6
  196.3 28.5 all-gather.8
  250.5 58.3 reduce-scatter.16
  311.3 37.9 reduce-scatter.14
  354.9 28.5 all-gather.10
  391.4 62.4 reduce-scatter.26
  471.7 66.7 reduce-scatter.24
  541.1 57.2 reduce-scatter.18
  602.5 69.5 reduce-scatter.22
  676.0 68.1 reduce-scatter.20
where the time goes:
time: 761 us; the launch traced here: 751 us
  waiting for transfers between devices  453 us (60%)
  matrix products  112 us (15%)
  local copies, waits for them, and re-layouts  73.3 us (10%)
  other arithmetic  55.6 us (7%)
  blocking collectives  40.3 us (5%)
  between operations  14.8 us (2%)
    reduce_scatter x1, waiting for transfers between devices, per_device(): lax.psum_scatter(grad_up, 'dp', scatter_dimension=0, tiled=True)  72.2 us
    reduce_scatter x1, waiting for transfers between devices, per_device(): lax.psum_scatter(jnp.dot(piece, out_proj, preferred_element_type=jnp.floa...  58.3 us
    reduce_scatter x1, waiting for transfers between devices, per_device(): lax.psum_scatter(jnp.einsum('cte,cde->td', piece, in_proj, preferred_elem...  58 us
    reduce_scatter x1, waiting for transfers between devices, per_device(): lax.psum_scatter(jnp.einsum('tf,df->td', piece, up_proj, preferred_elemen...  47 us
    unnamed x14, waiting for transfers between devices  45.7 us
    psum x1, blocking collectives, per_device(): lax.psum((jnp.stack([gain_first, gain_second]), jnp.stack([bias_first, bi...  40.3 us
    reduce_scatter x1, waiting for transfers between devices, per_device(): lax.psum_scatter(jnp.dot(piece, down_proj, preferred_element_type=jnp.flo...  37.8 us
    all_gather x1, waiting for transfers between devices, per_device(): lax.all_gather(normed.astype(jnp.bfloat16), 'tensor', axis=0, tiled=True)  31.3 us
  transfers between devices with their start and end apart: 12, of which 11 were waited for; matrix products, arithmetic and copies ran while one was open for 17% of the time, Pallas kernels for 0%

commit v1 on v0

--- a/solution.py
+++ b/solution.py
@@ -6,6 +6,23 @@
 HEAD_DIM = 64
 EPS = 1e-05
 NEG = -1e30
+
+
+def joined_along(pieces, dim):
+    pieces = jnp.moveaxis(pieces, 0, dim)
+    shape = pieces.shape
+    return pieces.reshape(*shape[:dim], shape[dim] * shape[dim + 1], *shape[dim + 2 :])
+
+
+def collected_by_bits(shard, axis):
+    size, position = (lax.axis_size(axis), lax.axis_index(axis))
+    blocks, bit = (shard[None], 1)
+    while bit < size:
+        theirs = lax.ppermute(blocks, axis, [(i, i ^ bit) for i in range(size)])
+        low = position & bit == 0
+        blocks = jnp.concatenate([jnp.where(low, blocks, theirs), jnp.where(low, theirs, blocks)])
+        bit *= 2
+    return blocks
 
 
 def layer_norm(values, gain, offset):
@@ -33,7 +50,8 @@
     positions = jnp.arange(length, dtype=jnp.int32)
     resid = tokens.astype(jnp.float32)
     normed, first_back = jax.vjp(layer_norm, resid, gains[0], biases[0])
-    normed_all = lax.all_gather(normed.astype(jnp.bfloat16), "tensor", axis=0, tiled=True)
+    x = normed.astype(jnp.bfloat16)
+    normed_all = joined_along(collected_by_bits(x, "tensor"), 0)
     projected = jnp.einsum(
         "td,cde->cte", normed_all, in_proj, preferred_element_type=jnp.float32
     ).astype(jnp.bfloat16)

time: 761 us -> 768 us (level)
  waiting for transfers between devices: 453 us -> 461 us
    ppermute x0 -> x2, waiting for transfers between devices: none -> 37.1 us  [collected_by_bits(): theirs = lax.ppermute(blocks, axis, [(i, i ^ bit) for i in range(size)])]
    all_gather x1 -> x0, waiting for transfers between devices: 31.3 us -> none  [per_device(): lax.all_gather(normed.astype(jnp.bfloat16), 'tensor', axis=0, tiled=True)]
    unnamed x68 -> x78, local copies, waits for them, and re-layouts: 18.8 us -> 21 us
    unnamed x14 -> x13, waiting for transfers between devices: 45.7 us -> 45.7 us
  transfers between devices with their start and end apart: 12 -> 13, of which waited for: 11 -> 12; matrix products, arithmetic and copies ran while one was open for 17% -> 16% of each run, Pallas kernels for 0% -> 0%
where the time goes in v1:
time: 768 us; the launch traced here: 761 us
  waiting for transfers between devices  461 us (60%)
  matrix products  110 us (14%)
  local copies, waits for them, and re-layouts  70.6 us (9%)
  other arithmetic  58.9 us (8%)
  blocking collectives  40.3 us (5%)
  between operations  14.5 us (2%)
    reduce_scatter x1, waiting for transfers between devices, per_device(): lax.psum_scatter(grad_up, 'dp', scatter_dimension=0, tiled=True)  72.2 us
    reduce_scatter x1, waiting for transfers between devices, per_device(): lax.psum_scatter(jnp.dot(piece, out_proj, preferred_element_type=jnp.floa...  59.9 us
    reduce_scatter x1, waiting for transfers between devices, per_device(): lax.psum_scatter(jnp.einsum('cte,cde->td', piece, in_proj, preferred_elem...  58.1 us
    reduce_scatter x1, waiting for transfers between devices, per_device(): lax.psum_scatter(jnp.einsum('tf,df->td', piece, up_proj, preferred_elemen...  47.2 us
    unnamed x13, waiting for transfers between devices  45.7 us
    psum x1, blocking collectives, per_device(): lax.psum((jnp.stack([gain_first, gain_second]), jnp.stack([bias_first, bi...  40.3 us
    reduce_scatter x1, waiting for transfers between devices, per_device(): lax.psum_scatter(jnp.dot(piece, down_proj, preferred_element_type=jnp.flo...  37.7 us
    ppermute x2, waiting for transfers between devices, collected_by_bits(): theirs = lax.ppermute(blocks, axis, [(i, i ^ bit) for i in range(size)])  37.1 us
  transfers between devices with their start and end apart: 13, of which 12 were waited for; matrix products, arithmetic and copies ran while one was open for 16% of the time, Pallas kernels for 0%

profile of v1, /device:TPU:0, one launch (start us, length us, event | category | flops | bytes accessed | tf_op | source)
XLA Modules:
  0.0 761.0 jit_solution(6106946598555535306)
XLA Ops:
  13.6 2.0 collective-permute-done
  15.7 1.7 broadcast_select_fusion.3
  18.7 2.9 collective-permute-start.1
  21.6 35.0 %collective-permute-done.1 = bf16[2,512,768]{2,1,0:T(8,128)(2,1)} collective-permute-done((bf16[2,512,768]{2,1,0:T(8,128)(2,1)}, bf16[2,512,768]{2,1,0:T(8,128)(2,1)}, u32[]{:S(2)}, u32[]{:S(2)}) %collective-permute-start.1) | collective-permute-done | bytes 1572896 | tf_op jit(solution)/shard_map/ppermute | solution.py:21
  56.6 1.6 broadcast_select_fusion.1
  59.4 2.0 fusion.55
  63.5 2.2 copy.49
  68.1 36.0 %while.58 = (s32[]{:T(128)}, bf16[2,2,512,192]{2,1,0,3:T(2,128)(2,1)}, f32[2,2,3,512]{3,2,1,0:T(4,128)}, bf16[2,2,512,192]{2,3,1,0:T(8,128)(2,1)}, bf16[2,1024,1...) while((s32[]{:T(128)}, ...), condition=%wide.region_7.8_spmd.clone, body=%wide.region_2.7_spmd.clone.sunk | while | flops 421625344 | bytes 24185224 | solution.py:91
  71.6 12.1 %while.61 = (s32[]{:T(128)}, bf16[2,512,192]{1,2,0:T(8,128)(2,1)S(1)}, f32[2,3,512]{2,1,0:T(4,128)}, s32[]{:T(128)}, s32[1024]{0:T(1024)S(1)}, /*index=5*/bf16[2...) while((s32[]{:T(128)}, ...), condition=%wide.region_6.6_spmd, body=%wide.region_3.5_spmd.sunk | while | flops 421625344 | bytes 21002412 | solution.py:89
  73.4 1.6 fusion.136
  75.1 2.0 fusion.137
  79.5 1.6 fusion.136
  81.1 2.0 fusion.137
  89.5 12.1 %while.61 = (s32[]{:T(128)}, bf16[2,512,192]{1,2,0:T(8,128)(2,1)S(1)}, f32[2,3,512]{2,1,0:T(4,128)}, s32[]{:T(128)}, s32[1024]{0:T(1024)S(1)}, /*index=5*/bf16[2...) while((s32[]{:T(128)}, ...), condition=%wide.region_6.6_spmd, body=%wide.region_3.5_spmd.sunk | while | flops 421625344 | bytes 21002412 | solution.py:89
  91.4 1.6 fusion.136
  93.0 2.0 fusion.137
  97.4 1.6 fusion.136
  99.0 2.0 fusion.137
  104.1 2.5 reshape.207
  106.7 4.9 fusion.56
  111.7 59.9 %reduce-scatter.13.cloned.1.call-done = f32[512,768]{1,0:T(8,128)} async-done(((f32[2048,768]{1,0:T(8,128)}), f32[512,768]{1,0:T(8,128)}) %reduce-scatter.13.cloned.1.call-update) | async-done | bytes 1572880 | tf_op jit(solution)/shard_map/reduce_scatter | solution.py:94
  171.6 1.6 fusion.52
  176.4 27.9 %all-gather.4.cloned.1.call-done = bf16[2048,768]{1,0:T(8,128)(2,1)} async-done(((bf16[512,768]{1,0:T(8,128)(2,1)}), bf16[2048,768]{1,0:T(8,128)(2,1)}) %all-gather.4.cloned.1.call-update) | async-done | bytes 3145744 | tf_op jit(solution)/shard_map/all_gather | solution.py:102
  204.3 7.5 fusion.57
  211.8 22.7 %all-gather.6.cloned.1.call-done = bf16[2048,768]{1,0:T(8,128)(2,1)} async-done(((bf16[512,768]{1,0:T(8,128)(2,1)}), bf16[2048,768]{1,0:T(8,128)(2,1)}) %all-gather.6.cloned.1.call-update) | async-done | bytes 3145744 | tf_op jit(solution)/shard_map/all_gather | solution.py:115
  234.5 19.3 %add_convert_fusion = (bf16[2048,768]{1,0:T(8,128)(2,1)S(1)}, f32[2048,768]{1,0:T(8,128)}) fusion(f32[2048,768]{1,0:T(8,128)} %fusion.57, bf16[2048,768]{1,0:T(8,128)(2,1)} %all-gather.6.cloned.1.call-done, bf16[768,768]{1,0:T(8,128)(2,1)S(1)} %copy-done), kind=kOutput, calls=%fused_computation.51 | convolution fusion | flops 2529165312 | bytes 20054016 | tf_op jit(solution)/shard_map/td,fd->tf/dot_general | solution.py:117
  253.8 1.7 copy-done.46
  255.5 4.5 fusion.58
  260.2 5.5 multiply_convert_fusion.1
  265.7 1.7 copy-done.19
  267.4 4.0 convolution_convert_fusion
  271.4 47.2 %reduce-scatter.17.cloned.1.call-done = f32[512,768]{1,0:T(8,128)} async-done(((f32[2048,768]{1,0:T(8,128)}), f32[512,768]{1,0:T(8,128)}) %reduce-scatter.17.cloned.1.call-update) | async-done | bytes 1572880 | tf_op jit(solution)/shard_map/reduce_scatter | solution.py:122
  318.6 2.6 multiply_reduce_fusion.1
  321.2 37.7 %reduce-scatter.15.cloned.1.call-done = bf16[512,768]{1,0:T(8,128)(2,1)} async-done(((bf16[2048,768]{1,0:T(8,128)(2,1)}), bf16[512,768]{1,0:T(8,128)(2,1)}) %reduce-scatter.15.cloned.1.call-update) | async-done | bytes 786448 | tf_op jit(solution)/shard_map/reduce_scatter | solution.py:108
  359.0 3.1 fusion.50
  364.6 28.6 %all-gather.8.cloned.1.call-done = bf16[2048,768]{1,0:T(8,128)(2,1)} async-done(((bf16[512,768]{1,0:T(8,128)(2,1)}), bf16[2048,768]{1,0:T(8,128)(2,1)}) %all-gather.8.cloned.1.call-update) | async-done | bytes 3145744 | tf_op jit(solution)/shard_map/all_gather | solution.py:130
  393.2 3.1 convolution_convert_fusion.1
  396.9 4.1 convolution_bitcast_fusion.2
  401.1 63.1 %while.60 = (s32[]{:T(128)}, bf16[2,1024,192]{2,1,0:T(8,128)(2,1)}, bf16[2,1024,192]{1,2,0:T(8,128)(2,1)}, bf16[2,1024,192]{1,2,0:T(8,128)(2,1)}, bf16[2,2,512,1...) while((s32[]{:T(128)}, bf16[2,1024,192]{2,1,0:T(8,128)(2,1)}, ...), condition=%wide.region_19.20_spmd.clone, body=%wide.region_15.19_spmd.clone.sunk | while | flops 1031798272 | bytes 92420848 | solution.py:188
  406.6 21.5 %while.62 = (s32[]{:T(128)}, f32[1024,3,64]{0,2,1:T(8,128)S(1)}, f32[1024,3,64]{0,2,1:T(8,128)}, bf16[2,512,192]{1,2,0:T(8,128)(2,1)}, bf16[2,512,192]{1,2,0:T(8...) while((s32[]{:T(128)}, f32[1024,3,64]{0,2,1:T(8,128)S(1)}, ...), condition=%wide.region_18.18_spmd.clone, body=%wide.region_16.17_spmd.clone.sunk | while | flops 1031405056 | bytes 63162644 | solution.py:178
  410.7 2.1 multiply_reduce_fusion.5
  412.8 1.7 multiply_convert_fusion.3
  421.5 2.1 multiply_reduce_fusion.5
  423.5 1.7 multiply_convert_fusion.3
  438.0 21.5 %while.62 = (s32[]{:T(128)}, f32[1024,3,64]{0,2,1:T(8,128)S(1)}, f32[1024,3,64]{0,2,1:T(8,128)}, bf16[2,512,192]{1,2,0:T(8,128)(2,1)}, bf16[2,512,192]{1,2,0:T(8...) while((s32[]{:T(128)}, f32[1024,3,64]{0,2,1:T(8,128)S(1)}, ...), condition=%wide.region_18.18_spmd.clone, body=%wide.region_16.17_spmd.clone.sunk | while | flops 1031405056 | bytes 63162644 | solution.py:178
  442.1 2.1 multiply_reduce_fusion.5
  444.1 1.7 multiply_convert_fusion.3
  452.8 2.1 multiply_reduce_fusion.5
  454.9 1.7 multiply_convert_fusion.3
  464.2 2.1 copy.59
  469.9 4.1 convolution_bitcast_fusion.1
  474.0 2.8 copy.62
  476.8 4.8 reshape.223
  481.7 4.6 convolution_bitcast_fusion
  486.4 7.0 fusion.60
  493.7 7.0 fusion.59
  502.0 1.6 copy.65
  503.6 44.8 %reduce-scatter.25.cloned.1.call-done = f32[96,576]{1,0:T(8,128)} async-done(((f32[768,576]{1,0:T(8,128)}), f32[96,576]{1,0:T(8,128)}) %reduce-scatter.25.cloned.1.call-update) | async-done | bytes 221200
  550.3 58.1 %reduce-scatter.19.cloned.1.call-done = f32[512,768]{1,0:T(8,128)} async-done(((f32[2048,768]{1,0:T(8,128)}), f32[512,768]{1,0:T(8,128)}) %reduce-scatter.19.cloned.1.call-update) | async-done | bytes 1572880 | tf_op jit(solution)/shard_map/reduce_scatter | solution.py:200
  608.5 2.0 fusion.49
  614.4 40.3 %all-reduce = (f32[2,768]{1,0:T(2,128)}, f32[2,768]{1,0:T(2,128)}) all-reduce(f32[2,768]{1,0:T(2,128)} %pad_maximum_fusion.5, f32[2,768]{1,0:T(2,128)} %pad_maximum_fusion.6), channel_id=1, replica_groups=mesh['dp'=8,'tensor'=4] {'dp','tensor'}, use_global_device_ids=true, to_apply=%region_29.30 | all-reduce | flops 3072 | bytes 24576 | tf_op jit(solution)/shard_map/psum | solution.py:208
  655.4 3.2 add_convert_fusion.1
  658.6 23.4 %reduce-scatter.23.cloned.1.call-done = f32[768,96]{0,1:T(8,128)} async-done(((f32[768,768]{0,1:T(8,128)}), f32[768,96]{0,1:T(8,128)}) %reduce-scatter.23.cloned.1.call-update) | async-done | bytes 294928 | tf_op jit(solution)/shard_map/reduce_scatter | solution.py:216
  682.0 72.2 %reduce-scatter.21.cloned.1.call-done = f32[96,768]{1,0:T(8,128)} async-done(((f32[768,768]{1,0:T(8,128)}), f32[96,768]{1,0:T(8,128)}) %reduce-scatter.21.cloned.1.call-update) | async-done | bytes 294928 | tf_op jit(solution)/shard_map/reduce_scatter | solution.py:215
  (311 shorter events, 99.5 us)
Async XLA Ops:
  7.2 227.4 %copy-start = (bf16[768,768]{1,0:T(8,128)(2,1)S(1)}, bf16[768,768]{1,0:T(8,128)(2,1)}, u32[]{:S(2)}) copy-start(bf16[768,768]{1,0:T(8,128)(2,1)} %param.22) | copy-start | bytes 3538948
  7.2 8.5 %copy-start.2 = (bf16[512,768]{1,0:T(8,128)(2,1)S(1)}, bf16[512,768]{1,0:T(8,128)(2,1)}, u32[]{:S(2)}) copy-start(bf16[512,768]{1,0:T(8,128)(2,1)} %param.17) | copy-start | bytes 2359300
  7.2 164.4 %reduce-scatter.13.cloned.1.call-start = ((), (), s32[]{:S(2)}) async-start(), calls=%async_computation.8 | async-start | bytes 7864320 | tf_op jit(solution)/shard_map/reduce_scatter | solution.py:94
  8.7 10.0 %copy-start.32 = (f32[512]{0:T(512)}, f32[512]{0:T(512)S(1)}, u32[]{:S(2)}) copy-start(f32[512]{0:T(512)S(1)} %broadcast_multiply_fusion.1) | copy-start | bytes 6148
  10.2 1.4 copy-start.37
  10.2 8.5 %copy-start.35 = (f32[512]{0:T(512)}, f32[512]{0:T(512)S(1)}, u32[]{:S(2)}) copy-start(f32[512]{0:T(512)S(1)} %fusion.44) | copy-start | bytes 6148
  11.6 7.1 copy-start.30
  13.1 2.6 collective-permute-start
  18.7 37.9 %collective-permute-start.1 = (bf16[2,512,768]{2,1,0:T(8,128)(2,1)}, bf16[2,512,768]{2,1,0:T(8,128)(2,1)}, u32[]{:S(2)}, u32[]{:S(2)}) collective-permute-start(bf16[2,512,768]{2,1,0:T(8,128)(2,1)} %pad_maximum_fusion.2), channel_id=1, source_target_pairs={{0,2},{1,3},{2,0},{3,1},{4,6},{5,7},{6,4},{7,5},{8,10},{9,11},{10,... | collective-permute-start | bytes 4718600 | tf_op jit(solution)/shard_map/ppermute | solution.py:21
  58.2 1.2 copy-start.44
  58.5 2.9 copy-start.18
  75.0 2.0 copy-start.27
  81.1 2.0 copy-start.27
  93.0 2.0 copy-start.27
  99.0 2.0 copy-start.27
  106.7 4.9 copy-start.16
  111.6 60.0 %copy-start.3 = (bf16[512,768]{1,0:T(8,128)(2,1)S(1)}, bf16[512,768]{1,0:T(8,128)(2,1)}, u32[]{:S(2)}) copy-start(bf16[512,768]{1,0:T(8,128)(2,1)} %param.17) | copy-start | bytes 2359300
  111.6 62.8 %copy-start.34 = (f32[768]{0:T(1024)S(1)}, f32[768]{0:T(1024)}, u32[]{:S(2)}) copy-start(f32[768]{0:T(1024)} %get-tuple-element.501) | copy-start | bytes 9220
  111.6 62.8 %copy-start.40 = (f32[768]{0:T(1024)S(1)}, f32[768]{0:T(1024)}, u32[]{:S(2)}) copy-start(f32[768]{0:T(1024)} %get-tuple-element.400) | copy-start | bytes 9220
  111.6 92.7 %all-gather.4.cloned.1.call-start = ((), (), s32[]{:S(2)}) async-start(), calls=%async_computation.9 | async-start | bytes 3932160 | tf_op jit(solution)/shard_map/all_gather | solution.py:102
  173.2 1.2 copy-start.5
  175.6 58.9 %all-gather.6.cloned.1.call-start = ((), (), s32[]{:S(2)}) async-start(), calls=%async_computation.11 | async-start | bytes 3932160 | tf_op jit(solution)/shard_map/all_gather | solution.py:115
  176.3 142.3 %reduce-scatter.17.cloned.1.call-start = ((), (), s32[]{:S(2)}) async-start(), calls=%async_computation.12 | async-start | bytes 7864320 | tf_op jit(solution)/shard_map/reduce_scatter | solution.py:122
  211.8 43.8 %copy-start.43 = (bf16[768,768]{1,0:T(8,128)(2,1)S(1)}, bf16[768,768]{1,0:T(8,128)(2,1)}, u32[]{:S(2)}) copy-start(bf16[768,768]{1,0:T(8,128)(2,1)} %param.21) | copy-start | bytes 3538948
  253.8 1.7 copy-start.46
  260.1 98.9 %reduce-scatter.15.cloned.1.call-start = ((), (), s32[]{:S(2)}) async-start(), calls=%async_computation.10 | async-start | bytes 3932160 | tf_op jit(solution)/shard_map/reduce_scatter | solution.py:108
  265.7 1.7 copy-start.19
  271.3 47.3 %copy-start.6 = (f32[512,768]{1,0:T(8,128)S(1)}, f32[512,768]{1,0:T(8,128)}, u32[]{:S(2)}) copy-start(f32[512,768]{1,0:T(8,128)} %copy-done.5) | copy-start | bytes 4718596
  271.4 121.8 %all-gather.8.cloned.1.call-start = ((), (), s32[]{:S(2)}) async-start(), calls=%async_computation.13 | async-start | bytes 3932160 | tf_op jit(solution)/shard_map/all_gather | solution.py:130
  321.2 42.1 %copy-start.15 = (bf16[512,768]{1,0:T(8,128)(2,1)S(1)}, bf16[512,768]{1,0:T(8,128)(2,1)}, u32[]{:S(2)}) copy-start(bf16[512,768]{1,0:T(8,128)(2,1)} %param.25) | copy-start | bytes 2359300
  362.1 1.2 copy-start.10
  362.1 31.1 %copy-start.29 = (bf16[192,768]{1,0:T(8,128)(2,1)S(1)}, bf16[192,768]{1,0:T(8,128)(2,1)}, u32[]{:S(2)}) copy-start(bf16[192,768]{1,0:T(8,128)(2,1)} %param.20) | copy-start | bytes 884740
  362.1 34.1 %copy-start.39 = (f32[512]{0:T(512)}, f32[512]{0:T(512)S(1)}, u32[]{:S(2)}) copy-start(f32[512]{0:T(512)S(1)} %negate_multiply_fusion.2) | copy-start | bytes 6148
  364.5 137.5 %reduce-scatter.27.cloned.1.call-start = ((), (), s32[]{:S(2)}) async-start(), calls=%async_computation.18 | async-start | bytes 884736
  364.6 32.3 %copy-start.17 = (bf16[2048,192]{0,1:T(8,128)(2,1)S(1)}, bf16[2048,192]{0,1:T(8,128)(2,1)}, u32[]{:S(2)}) copy-start(bf16[2048,192]{0,1:T(8,128)(2,1)} %copy-done.16) | copy-start | bytes 2359300
  401.0 147.4 %reduce-scatter.25.cloned.1.call-start = ((), (), s32[]{:S(2)}) async-start(), calls=%async_computation.17 | async-start | bytes 2211840
  401.5 5.1 copy-start.13
  410.7 2.1 copy-start.8
  421.4 2.1 copy-start.8
  428.1 3.5 copy-start.21
  429.4 2.2 copy-start.23
  429.5 3.4 copy-start.14
  432.9 5.1 copy-start.13
  442.0 2.1 copy-start.8
  452.8 2.1 copy-start.8
  459.4 3.5 copy-start.21
  460.7 2.2 copy-start.23
  460.8 3.4 copy-start.14
  464.2 3.6 copy-start.20
  464.2 4.3 copy-start.25
  476.8 4.9 copy-start.26
  476.8 4.9 copy-start.45
  481.6 126.8 %reduce-scatter.19.cloned.1.call-start = ((), (), s32[]{:S(2)}) async-start(), calls=%async_computation.14 | async-start | bytes 7864320 | tf_op jit(solution)/shard_map/reduce_scatter | solution.py:200
  486.3 195.7 %reduce-scatter.23.cloned.1.call-start = ((), (), s32[]{:S(2)}) async-start(), calls=%async_computation.16 | async-start | bytes 2654208 | tf_op jit(solution)/shard_map/reduce_scatter | solution.py:216
  493.5 7.4 copy-start.42
  493.5 7.9 %copy-start.41 = (f32[768]{0:T(1024)S(1)}, f32[768]{0:T(1024)}, u32[]{:S(2)}) copy-start(f32[768]{0:T(1024)} %get-tuple-element.397) | copy-start | bytes 9220
  493.5 260.8 %reduce-scatter.21.cloned.1.call-start = ((), (), s32[]{:S(2)}) async-start(), calls=%async_computation.15 | async-start | bytes 2654208 | tf_op jit(solution)/shard_map/reduce_scatter | solution.py:215
  500.8 107.7 %copy-start.4 = (bf16[512,768]{1,0:T(8,128)(2,1)S(1)}, bf16[512,768]{1,0:T(8,128)(2,1)}, u32[]{:S(2)}) copy-start(bf16[512,768]{1,0:T(8,128)(2,1)} %param.17) | copy-start | bytes 2359300
  500.8 107.7 %copy-start.31 = (f32[768]{0:T(1024)S(1)}, f32[768]{0:T(1024)}, u32[]{:S(2)}) copy-start(f32[768]{0:T(1024)} %copy-done.30) | copy-start | bytes 9220
  500.8 107.7 %copy-start.33 = (f32[512]{0:T(512)S(1)}, f32[512]{0:T(512)}, u32[]{:S(2)}) copy-start(f32[512]{0:T(512)} %copy-done.32) | copy-start | bytes 6148
  500.8 109.7 %copy-start.38 = (f32[512]{0:T(512)S(1)}, f32[512]{0:T(512)}, u32[]{:S(2)}) copy-start(f32[512]{0:T(512)} %copy-done.37) | copy-start | bytes 6148
  500.8 109.7 %copy-start.36 = (f32[512]{0:T(512)S(1)}, f32[512]{0:T(512)}, u32[]{:S(2)}) copy-start(f32[512]{0:T(512)} %copy-done.35) | copy-start | bytes 6148
  608.5 2.0 copy-start.9
  610.5 143.8 %copy-start.1 = (bf16[768,768]{1,0:T(8,128)(2,1)S(1)}, bf16[768,768]{1,0:T(8,128)(2,1)}, u32[]{:S(2)}) copy-start(bf16[768,768]{1,0:T(8,128)(2,1)} %param.22) | copy-start | bytes 3538948
  (20 other events, 18.1 us)
Sparse Core Ops, SparseCore 0:
  111.7 59.8 reduce-scatter.12
  175.7 28.5 all-gather.3
  206.0 28.5 all-gather.5
  260.2 58.3 reduce-scatter.16
  321.0 37.9 reduce-scatter.14
  364.6 28.5 all-gather.7
  401.1 62.3 reduce-scatter.26
  481.8 66.6 reduce-scatter.24
  551.2 57.2 reduce-scatter.18
  612.4 69.5 reduce-scatter.22
  686.1 68.1 reduce-scatter.20
